TPU v7x, 32 devices: a whole 2x2x4 slice. The times are simulated.
32 devices in a mesh: grp: 2 (over x), seq: 16 (over z, y, core).
Axes of the slice: x: 2, y: 2, z: 4, core: 2. Of those that a mesh axis runs over, the one named last changes fastest.
Arguments:
- queries: bfloat16 [128, 5120], P(('grp', 'seq')), parts along dimension 0
- keys: bfloat16 [16384, 5120], P(('grp', 'seq')), parts along dimension 0
- values: bfloat16 [16384, 5120], P(('grp', 'seq')), parts along dimension 0, may hold values from -6 to 6
- gain: float32 [5120], replicated, may hold values from 0.1 to 1.9
Outputs:
- window_out: bfloat16 [128, 5120], P(('grp', 'seq')), parts along dimension 0
There are 2 independent parts, one for each index of `grp`. A program takes and returns all parts, laid end to end along the dimension named above; an argument that names none is the same for every part. Nothing has to cross between parts.
All inputs are finite; a program needn't handle non-finite values.
Results may differ from a plain program's by a relative error of at most 0.001.
Values may be sent and summed in bfloat16 or wider, within the bound.
No kernel may reach another device: no remote copies, remote signals or barrier semaphores. Data moves between devices by JAX's collectives and lax.ppermute only.
A program may use at most 128 MiB of HBM per device.

v0:
```python
import math

import jax
import jax.numpy as jnp
from jax import lax
from jax.sharding import PartitionSpec as P

HEADS = 40
HDIM = 128


def split_groups(matrix):
    row_count = matrix.shape[0]
    group_count = HEADS // 8
    return matrix.reshape(row_count, group_count, 8, HDIM).transpose(1, 0, 2, 3)


def group_scores(query_part, key_part):
    score_scale = 1.0 / math.sqrt(HDIM)
    return (
        jnp.einsum("qhd,thd->hqt", query_part, key_part, preferred_element_type=jnp.float32)
        * score_scale
    )


def weighted_values(weights, value_part):
    return jnp.einsum(
        "hqt,thd->qhd", weights, value_part.astype(jnp.float32), precision=lax.Precision.HIGHEST
    )


def shards(queries, keys, values, gain):
    all_queries = lax.all_gather(queries, "seq", axis=0, tiled=True)
    window_rows = all_queries.shape[0]
    rows_here = queries.shape[0]
    query_groups = split_groups(all_queries)
    key_groups = split_groups(keys)
    value_groups = split_groups(values)

    def partial_of(members):
        query_part, key_part, value_part = members
        scores = group_scores(query_part, key_part)
        max_part = jnp.max(scores, axis=2)
        weights = jnp.exp(scores - max_part[:, :, None])
        return (weighted_values(weights, value_part), max_part, jnp.sum(weights, axis=2))

    numerator, local_max, denominator = lax.map(
        partial_of, (query_groups, key_groups, value_groups)
    )
    numer_rows = numerator.transpose(1, 0, 2, 3).reshape(window_rows, HEADS * HDIM)
    max_rows = local_max.reshape(HEADS, window_rows).transpose(1, 0)
    denom_rows = denominator.reshape(HEADS, window_rows).transpose(1, 0)
    numer_in, max_in, denom_in = (
        lax.all_to_all(numer_rows, "seq", split_axis=0, concat_axis=0, tiled=True),
        lax.all_to_all(max_rows, "seq", split_axis=0, concat_axis=0, tiled=True),
        lax.all_to_all(denom_rows, "seq", split_axis=0, concat_axis=0, tiled=True),
    )
    peer_count = lax.axis_size("seq")
    numer_in = numer_in.reshape(peer_count, rows_here, HEADS, HDIM)
    max_in = max_in.reshape(peer_count, rows_here, HEADS)
    denom_in = denom_in.reshape(peer_count, rows_here, HEADS)
    row_peak = jnp.max(max_in, axis=0)
    rescale = jnp.exp(max_in - row_peak[None])
    total_denom = jnp.sum(rescale * denom_in, axis=0)
    summed = jnp.sum(rescale[:, :, :, None] * numer_in, axis=0)
    attended = summed / total_denom[:, :, None]
    flattened = attended.reshape(rows_here, HEADS * HDIM)
    root_mean = jnp.sqrt(jnp.mean(flattened * flattened, axis=1, keepdims=True) + 1e-06)
    return (flattened / root_mean * gain).astype(jnp.bfloat16)


def solution(mesh):
    in_specs = (P(("grp", "seq"), None), P(("grp", "seq"), None), P(("grp", "seq"), None), P())
    out_specs = P(("grp", "seq"), None)
    return jax.shard_map(shards, mesh=mesh, in_specs=in_specs, out_specs=out_specs, check_vma=False)
```

profile of v0, /device:TPU:13, one launch (start us, length us, event | category | flops | bytes accessed | tf_op | source)
XLA Modules:
  0.0 119.2 jit_solution(9282598131096698049)
XLA Ops:
  0.0 7.9 %copy.23 = bf16[512,5120]{0,1:T(8,128)(2,1)} copy(bf16[512,5120]{1,0:T(8,128)(2,1)} %param.7) | data formatting | bytes 10485760 | tf_op args[1]
  7.9 8.0 %copy.22 = bf16[512,5120]{0,1:T(8,128)(2,1)} copy(bf16[512,5120]{1,0:T(8,128)(2,1)} %param.8) | data formatting | bytes 10485760 | tf_op args[2]
  15.9 17.4 %all-gather = bf16[16,4,5120]{2,1,0:T(4,128)(2,1)S(1)} all-gather(bf16[1,4,5120]{2,1,0:T(4,128)(2,1)S(1)} %bitcast.75), channel_id=1, replica_groups=mesh['grp'=2,'seq'=16] {'seq'}, dimensions={0}, use_global_device_ids=true | all-gather | bytes 696320 | tf_op jit(solution)/shard_map/all_gather | solution.py:33
  33.6 22.7 %while.14 = (s32[]{:T(128)}, f32[5,64,8,128]{3,1,2,0:T(8,128)S(1)}, f32[5,8,64]{2,1,0:T(8,128)S(1)}, f32[5,8,64]{2,1,0:T(8,128)S(1)}, bf16[5,512,8,128]{1,3,2,0:...) while((s32[]{:T(128)}, f32[5,64,8,128]{3,1,2,0:T(8,128)S(1)}, ...), condition=%wide.region_3.4_spmd, body=%wide.region_0.3_spmd.sunk | while | flops 471071744 | bytes 5926493 | solution.py:47
  33.6 1.6 %fusion.18 = (f32[8,64]{1,0:T(8,128)S(1)}, f32[8,64,512]{2,1,0:T(8,128)S(1)}) fusion(bf16[5,512,8,128]{1,3,2,0:T(8,128)(2,1)} %get-tuple-element.161, s32[]{:T(128)} %get-tuple-element.147, bf16[1,64,8,128]{3,2,0,1:T(8,128)(2,1)S(1)} %constant_dynamic-slice_fusion.2), kind=kOutput, calls=%fused_computation.27.clone.1 | convolution fusion | flops 67632640 | bytes 2230784 | tf_op jit(solution)/shard_map/while/body/eval_jaxpr/qhd,thd->hqt/dot_general | solution.py:21
  35.6 2.5 %fusion.19 = f32[5,64,8,128]{3,1,2,0:T(8,128)S(1)} fusion(f32[5,64,8,128]{3,1,2,0:T(8,128)S(1)} %get-tuple-element.148, s32[]{:T(128)} %get-tuple-element.147, bf16[5,512,8,128]{1,3,2,0:T(8,128)(2,1)} %get-tuple-element.159, f32[8,64,512]{2,1,0:T(8,128)S(1)} %get-tuple-element.135, f32[8,64]{1,0:T(8,128)S(1)} %get-tuple-element.136), kind=kOutput, calls=%fused_computation.2.clone.1 | convolution fusion | flops 402915328 | bytes 2364416 | tf_op jit(solution)/shard_map/while/body/eval_jaxpr/hqt,thd->qhd/dot_general | solution.py:27
  38.1 1.6 %fusion.18 = (f32[8,64]{1,0:T(8,128)S(1)}, f32[8,64,512]{2,1,0:T(8,128)S(1)}) fusion(bf16[5,512,8,128]{1,3,2,0:T(8,128)(2,1)} %get-tuple-element.161, s32[]{:T(128)} %get-tuple-element.147, bf16[1,64,8,128]{3,2,0,1:T(8,128)(2,1)S(1)} %constant_dynamic-slice_fusion.2), kind=kOutput, calls=%fused_computation.27.clone.1 | convolution fusion | flops 67632640 | bytes 2230784 | tf_op jit(solution)/shard_map/while/body/eval_jaxpr/qhd,thd->hqt/dot_general | solution.py:21
  40.1 2.5 %fusion.19 = f32[5,64,8,128]{3,1,2,0:T(8,128)S(1)} fusion(f32[5,64,8,128]{3,1,2,0:T(8,128)S(1)} %get-tuple-element.148, s32[]{:T(128)} %get-tuple-element.147, bf16[5,512,8,128]{1,3,2,0:T(8,128)(2,1)} %get-tuple-element.159, f32[8,64,512]{2,1,0:T(8,128)S(1)} %get-tuple-element.135, f32[8,64]{1,0:T(8,128)S(1)} %get-tuple-element.136), kind=kOutput, calls=%fused_computation.2.clone.1 | convolution fusion | flops 402915328 | bytes 2364416 | tf_op jit(solution)/shard_map/while/body/eval_jaxpr/hqt,thd->qhd/dot_general | solution.py:27
  42.7 1.6 %fusion.18 = (f32[8,64]{1,0:T(8,128)S(1)}, f32[8,64,512]{2,1,0:T(8,128)S(1)}) fusion(bf16[5,512,8,128]{1,3,2,0:T(8,128)(2,1)} %get-tuple-element.161, s32[]{:T(128)} %get-tuple-element.147, bf16[1,64,8,128]{3,2,0,1:T(8,128)(2,1)S(1)} %constant_dynamic-slice_fusion.2), kind=kOutput, calls=%fused_computation.27.clone.1 | convolution fusion | flops 67632640 | bytes 2230784 | tf_op jit(solution)/shard_map/while/body/eval_jaxpr/qhd,thd->hqt/dot_general | solution.py:21
  44.7 2.5 %fusion.19 = f32[5,64,8,128]{3,1,2,0:T(8,128)S(1)} fusion(f32[5,64,8,128]{3,1,2,0:T(8,128)S(1)} %get-tuple-element.148, s32[]{:T(128)} %get-tuple-element.147, bf16[5,512,8,128]{1,3,2,0:T(8,128)(2,1)} %get-tuple-element.159, f32[8,64,512]{2,1,0:T(8,128)S(1)} %get-tuple-element.135, f32[8,64]{1,0:T(8,128)S(1)} %get-tuple-element.136), kind=kOutput, calls=%fused_computation.2.clone.1 | convolution fusion | flops 402915328 | bytes 2364416 | tf_op jit(solution)/shard_map/while/body/eval_jaxpr/hqt,thd->qhd/dot_general | solution.py:27
  47.2 1.6 %fusion.18 = (f32[8,64]{1,0:T(8,128)S(1)}, f32[8,64,512]{2,1,0:T(8,128)S(1)}) fusion(bf16[5,512,8,128]{1,3,2,0:T(8,128)(2,1)} %get-tuple-element.161, s32[]{:T(128)} %get-tuple-element.147, bf16[1,64,8,128]{3,2,0,1:T(8,128)(2,1)S(1)} %constant_dynamic-slice_fusion.2), kind=kOutput, calls=%fused_computation.27.clone.1 | convolution fusion | flops 67632640 | bytes 2230784 | tf_op jit(solution)/shard_map/while/body/eval_jaxpr/qhd,thd->hqt/dot_general | solution.py:21
  49.2 2.5 %fusion.19 = f32[5,64,8,128]{3,1,2,0:T(8,128)S(1)} fusion(f32[5,64,8,128]{3,1,2,0:T(8,128)S(1)} %get-tuple-element.148, s32[]{:T(128)} %get-tuple-element.147, bf16[5,512,8,128]{1,3,2,0:T(8,128)(2,1)} %get-tuple-element.159, f32[8,64,512]{2,1,0:T(8,128)S(1)} %get-tuple-element.135, f32[8,64]{1,0:T(8,128)S(1)} %get-tuple-element.136), kind=kOutput, calls=%fused_computation.2.clone.1 | convolution fusion | flops 402915328 | bytes 2364416 | tf_op jit(solution)/shard_map/while/body/eval_jaxpr/hqt,thd->qhd/dot_general | solution.py:27
  51.7 1.6 %fusion.18 = (f32[8,64]{1,0:T(8,128)S(1)}, f32[8,64,512]{2,1,0:T(8,128)S(1)}) fusion(bf16[5,512,8,128]{1,3,2,0:T(8,128)(2,1)} %get-tuple-element.161, s32[]{:T(128)} %get-tuple-element.147, bf16[1,64,8,128]{3,2,0,1:T(8,128)(2,1)S(1)} %constant_dynamic-slice_fusion.2), kind=kOutput, calls=%fused_computation.27.clone.1 | convolution fusion | flops 67632640 | bytes 2230784 | tf_op jit(solution)/shard_map/while/body/eval_jaxpr/qhd,thd->hqt/dot_general | solution.py:21
  53.7 2.5 %fusion.19 = f32[5,64,8,128]{3,1,2,0:T(8,128)S(1)} fusion(f32[5,64,8,128]{3,1,2,0:T(8,128)S(1)} %get-tuple-element.148, s32[]{:T(128)} %get-tuple-element.147, bf16[5,512,8,128]{1,3,2,0:T(8,128)(2,1)} %get-tuple-element.159, f32[8,64,512]{2,1,0:T(8,128)S(1)} %get-tuple-element.135, f32[8,64]{1,0:T(8,128)S(1)} %get-tuple-element.136), kind=kOutput, calls=%fused_computation.2.clone.1 | convolution fusion | flops 402915328 | bytes 2364416 | tf_op jit(solution)/shard_map/while/body/eval_jaxpr/hqt,thd->qhd/dot_general | solution.py:27
  57.0 10.2 %all-to-all-start = ((f32[16,1,160]{2,1,0:T(1,128)}), f32[16,1,160]{2,1,0:T(1,128)S(1)}, u32[]{:S(2)}, u32[]{:S(2)}) async-start(f32[16,1,160]{2,1,0:T(1,128)} %reshape.63), calls=%async_computation | async-start | bytes 32768 | tf_op jit(solution)/shard_map/all_to_all | solution.py:55
  68.0 3.4 %all-to-all-done = f32[16,1,160]{2,1,0:T(1,128)S(1)} async-done(((f32[16,1,160]{2,1,0:T(1,128)}), f32[16,1,160]{2,1,0:T(1,128)S(1)}, u32[]{:S(2)}, u32[]{:S(2)}) %all-to-all-start) | async-done | bytes 10272 | tf_op jit(solution)/shard_map/all_to_all | solution.py:55
  71.4 5.8 %all-to-all-start.2 = ((f32[16,1,160]{2,1,0:T(1,128)}), f32[16,1,160]{2,1,0:T(1,128)S(1)}, u32[]{:S(2)}, u32[]{:S(2)}) async-start(f32[16,1,160]{2,1,0:T(1,128)} %reshape.65), calls=%async_computation.2 | async-start | bytes 32768 | tf_op jit(solution)/shard_map/all_to_all | solution.py:56
  77.2 0.8 copy.28
  78.0 1.5 %all_to_all.20 = f32[16,4,5120]{2,1,0:T(4,128)} reshape(f32[64,5,8,128]{3,2,1,0:T(8,128)S(1)} %copy.28) | data formatting | bytes 2621440 | tf_op jit(solution)/shard_map/all_to_all | solution.py:54
  79.5 1.9 %all-to-all-done.2 = f32[16,1,160]{2,1,0:T(1,128)S(1)} async-done(((f32[16,1,160]{2,1,0:T(1,128)}), f32[16,1,160]{2,1,0:T(1,128)S(1)}, u32[]{:S(2)}, u32[]{:S(2)}) %all-to-all-start.2) | async-done | bytes 10272 | tf_op jit(solution)/shard_map/all_to_all | solution.py:56
  81.4 6.0 %all-to-all-start.1 = ((f32[16,4,5120]{2,1,0:T(4,128)}), f32[16,4,5120]{2,1,0:T(4,128)S(1)}, u32[]{:S(2)}, u32[]{:S(2)}) async-start(f32[16,4,5120]{2,1,0:T(4,128)} %all_to_all.20), calls=%async_computation.1 | async-start | bytes 2621440 | tf_op jit(solution)/shard_map/all_to_all | solution.py:54
  89.5 1.5 %mul.32 = f32[16,4,40,128]{3,2,1,0:T(8,128)} broadcast(f32[16,4,40]{2,1,0:T(4,128)S(1)} %get-tuple-element.83), dimensions={0,1,2} | broadcast | bytes 1320960 | tf_op jit(solution)/shard_map/mul | solution.py:65
  91.0 1.7 %mul.33 = f32[16,4,5120]{2,1,0:T(4,128)S(1)} reshape(f32[16,4,40,128]{3,2,1,0:T(8,128)} %mul.32) | data formatting | bytes 2621440 | tf_op jit(solution)/shard_map/mul | solution.py:65
  92.8 25.1 %all-to-all-done.1 = f32[16,4,5120]{2,1,0:T(4,128)S(1)} async-done(((f32[16,4,5120]{2,1,0:T(4,128)}), f32[16,4,5120]{2,1,0:T(4,128)S(1)}, u32[]{:S(2)}, u32[]{:S(2)}) %all-to-all-start.1) | async-done | bytes 1310752 | tf_op jit(solution)/shard_map/all_to_all | solution.py:54
  (39 shorter events, 7.3 us)
Async XLA Ops:
  7.9 8.0 %copy-start = (bf16[4,5120]{1,0:T(4,128)(2,1)S(1)}, bf16[4,5120]{1,0:T(4,128)(2,1)}, u32[]{:S(2)}) copy-start(bf16[4,5120]{1,0:T(4,128)(2,1)} %param.6) | copy-start | bytes 122884
  57.0 14.4 %all-to-all-start = ((f32[16,1,160]{2,1,0:T(1,128)}), f32[16,1,160]{2,1,0:T(1,128)S(1)}, u32[]{:S(2)}, u32[]{:S(2)}) async-start(f32[16,1,160]{2,1,0:T(1,128)} %reshape.63), calls=%async_computation | async-start | bytes 32768 | tf_op jit(solution)/shard_map/all_to_all | solution.py:55
  71.4 10.0 %all-to-all-start.2 = ((f32[16,1,160]{2,1,0:T(1,128)}), f32[16,1,160]{2,1,0:T(1,128)S(1)}, u32[]{:S(2)}, u32[]{:S(2)}) async-start(f32[16,1,160]{2,1,0:T(1,128)} %reshape.65), calls=%async_computation.2 | async-start | bytes 32768 | tf_op jit(solution)/shard_map/all_to_all | solution.py:56
  81.4 36.6 %all-to-all-start.1 = ((f32[16,4,5120]{2,1,0:T(4,128)}), f32[16,4,5120]{2,1,0:T(4,128)S(1)}, u32[]{:S(2)}, u32[]{:S(2)}) async-start(f32[16,4,5120]{2,1,0:T(4,128)} %all_to_all.20), calls=%async_computation.1 | async-start | bytes 2621440 | tf_op jit(solution)/shard_map/all_to_all | solution.py:54
  92.8 25.7 %copy-start.1 = (f32[5120]{0:T(1024)S(1)}, f32[5120]{0:T(1024)}, u32[]{:S(2)}) copy-start(f32[5120]{0:T(1024)} %param.9) | copy-start | bytes 61444
where the time goes:
time: 120 us; the launch traced here: 119 us
  waiting for transfers between devices  30.4 us (25%)
  local copies, waits for them, and re-layouts  24.1 us (20%)
  starting transfers between devices  22 us (18%)
  matrix products  20.5 us (17%)
  blocking collectives  17.4 us (14%)
  other arithmetic  4.56 us (4%)
    all_to_all x1, waiting for transfers between devices, shards(): lax.all_to_all(numer_rows, 'seq', split_axis=0, concat_axis=0, tiled=True)  25.1 us
    unnamed x11, local copies, waits for them, and re-layouts  17.6 us
    all_gather x1, blocking collectives, shards(): all_queries = lax.all_gather(queries, 'seq', axis=0, tiled=True)  17.4 us
    dot_general x5, matrix products, weighted_values(): jnp.einsum('hqt,thd->qhd', weights, value_part.astype(jnp.float32), preci...  12.5 us
    all_to_all x1, starting transfers between devices, shards(): lax.all_to_all(max_rows, 'seq', split_axis=0, concat_axis=0, tiled=True)  10.2 us
    dot_general x5, matrix products, group_scores(): jnp.einsum('qhd,thd->hqt', query_part, key_part, preferred_element_type=j...  8.02 us
    all_to_all x1, starting transfers between devices, shards(): lax.all_to_all(numer_rows, 'seq', split_axis=0, concat_axis=0, tiled=True)  5.99 us
    all_to_all x1, starting transfers between devices, shards(): lax.all_to_all(denom_rows, 'seq', split_axis=0, concat_axis=0, tiled=True)  5.78 us
  transfers between devices with their start and end apart: 3, of which 3 were waited for; matrix products, arithmetic and copies ran while one was open for 6% of the time, Pallas kernels for 0%

commit v1 on v0

v1 whole, which is shorter than its diff:
```python
import math

import jax
import jax.numpy as jnp
from jax import lax
from jax.experimental import pallas as pl
from jax.experimental.pallas import tpu as pltpu
from jax.sharding import PartitionSpec as P

HDIM = 128
EXP2_SCALE = math.log2(math.e) / math.sqrt(HDIM)
VMEM_SPEC = pl.BlockSpec(memory_space=pltpu.VMEM)


def head_columns(head):
    return pl.ds(pl.multiple_of(head * HDIM, HDIM), HDIM)


def attend_kernel(query_ref, key_ref, value_ref, keep_ref, send_ref):
    rows, width = query_ref.shape
    half = rows // 2
    heads = width // HDIM
    lane = lax.broadcasted_iota(jnp.int32, (rows, HDIM), 1)

    def one_head(head, carry):
        maxima, denominators = carry
        columns = head_columns(head)
        dots = lax.dot_general(
            query_ref[:, columns],
            key_ref[:, columns],
            (((1,), (1,)), ((), ())),
            preferred_element_type=jnp.float32,
        )
        peak = jnp.max(dots, axis=1, keepdims=True)
        weights = jnp.exp2((dots - peak) * EXP2_SCALE)
        total = jnp.sum(weights, axis=1, keepdims=True)
        coarse = weights.astype(jnp.bfloat16)
        fine = (weights - coarse.astype(jnp.float32)).astype(jnp.bfloat16)
        sums = jnp.dot(
            jnp.concatenate([coarse, fine], axis=0),
            value_ref[:, columns],
            preferred_element_type=jnp.float32,
        )
        numerator = sums[:rows] + sums[rows:]
        keep_ref[:, columns] = numerator[:half]
        send_ref[:, columns] = numerator[half:]
        return jnp.where(lane == head, peak, maxima), jnp.where(lane == head, total, denominators)

    zeros = jnp.zeros((rows, HDIM), jnp.float32)
    maxima, denominators = lax.fori_loop(0, heads, one_head, (zeros, zeros), unroll=4)
    for ref, first in ((keep_ref, 0), (send_ref, half)):
        ref[:, width : width + HDIM] = maxima[first : first + half]
        ref[:, width + HDIM :] = denominators[first : first + half]


def merged_scales(here, there, width):
    max_here, max_there = here[:, width : width + HDIM], there[:, width : width + HDIM]
    maxima = jnp.maximum(max_here, max_there)
    scale_here = jnp.exp2((max_here - maxima) * EXP2_SCALE)
    scale_there = jnp.exp2((max_there - maxima) * EXP2_SCALE)
    denominators = scale_here * here[:, width + HDIM :] + scale_there * there[:, width + HDIM :]
    return maxima, denominators, scale_here, scale_there


def merge_kernel(here_ref, there_ref, keep_ref, send_ref):
    rows, padded = here_ref.shape
    width = padded - 2 * HDIM
    half = rows // 2
    maxima, denominators, scale_here, scale_there = merged_scales(here_ref, there_ref, width)
    for head in range(width // HDIM):
        columns = slice(head * HDIM, (head + 1) * HDIM)
        lane = slice(head, head + 1)
        merged = scale_here[:, lane] * here_ref[:, columns] + scale_there[:, lane] * there_ref[:, columns]
        keep_ref[:, columns] = merged[:half]
        send_ref[:, columns] = merged[half:]
    for ref, first in ((keep_ref, 0), (send_ref, half)):
        ref[:, width : width + HDIM] = maxima[first : first + half]
        ref[:, width + HDIM :] = denominators[first : first + half]


def finish_kernel(here_ref, there_ref, gain_ref, out_ref):
    rows, width = out_ref.shape
    _, denominators, scale_here, scale_there = merged_scales(here_ref, there_ref, width)
    scale_here = scale_here / denominators
    scale_there = scale_there / denominators
    squares = jnp.zeros((rows, HDIM), jnp.float32)
    attended = []
    for head in range(width // HDIM):
        columns = slice(head * HDIM, (head + 1) * HDIM)
        lane = slice(head, head + 1)
        block = scale_here[:, lane] * here_ref[:, columns] + scale_there[:, lane] * there_ref[:, columns]
        squares = squares + block * block
        attended.append(block)
    mean = jnp.sum(squares, axis=1, keepdims=True) / width
    inverse = 1.0 / jnp.sqrt(mean + 1e-06)
    for head, block in enumerate(attended):
        columns = slice(head * HDIM, (head + 1) * HDIM)
        out_ref[:, columns] = (block * inverse * gain_ref[:, columns]).astype(out_ref.dtype)


def call(kernel, out_shape, operands, flops=0, name=None):
    outs = out_shape if isinstance(out_shape, (tuple, list)) else [out_shape]
    size = sum(math.prod(a.shape) * a.dtype.itemsize for a in (*operands, *outs))
    return pl.pallas_call(
        kernel,
        out_shape=out_shape,
        in_specs=[VMEM_SPEC] * len(operands),
        out_specs=jax.tree.map(lambda _: VMEM_SPEC, out_shape),
        cost_estimate=pl.CostEstimate(flops=flops, bytes_accessed=size, transcendentals=0),
        compiler_params=pltpu.CompilerParams(vmem_limit_bytes=12 << 20),
        name=name,
    )(*operands)


def exchange(array, mask, size):
    return lax.ppermute(array, "seq", [(i, i ^ mask) for i in range(size)])


def shards(queries, keys, values, gain):
    peers = lax.axis_size("seq")
    masks = [1 << bit for bit in range(peers.bit_length() - 1)]
    rows, width = queries.shape
    window = queries
    for mask in reversed(masks):
        window = jnp.concatenate([window, exchange(window, mask, peers)], axis=0)

    def pair(count):
        return (jax.ShapeDtypeStruct((count, width + 2 * HDIM), jnp.float32),) * 2

    flops = 4 * window.shape[0] * keys.shape[0] * width
    keep, send = call(attend_kernel, pair(window.shape[0] // 2), (window, keys, values), flops, "attend")
    for mask in masks[:-1]:
        arrived = exchange(send, mask, peers)
        keep, send = call(merge_kernel, pair(keep.shape[0] // 2), (keep, arrived), 0, "merge")
    arrived = exchange(send, masks[-1], peers)
    out = jax.ShapeDtypeStruct((rows, width), jnp.bfloat16)
    return call(finish_kernel, out, (keep, arrived, gain.reshape(1, width)), 0, "finish")


def solution(mesh):
    spec = P(("grp", "seq"), None)
    return jax.shard_map(shards, mesh=mesh, in_specs=(spec, spec, spec, P()), out_specs=spec, check_vma=False)
```

time: 120 us -> 64.7 us (0.54)
  the two profiles are of different devices: /device:TPU:13 before, /device:TPU:0 now
where the time goes in v1:
time: 64.7 us; the launch traced here: 64.3 us
  waiting for transfers between devices  28 us (43%)
  Pallas kernels  13.9 us (21%)
  starting transfers between devices  13.7 us (21%)
  local copies, waits for them, and re-layouts  6.02 us (9%)
  other arithmetic  2.52 us (4%)
    ppermute x8, waiting for transfers between devices, exchange(): return lax.ppermute(array, 'seq', [(i, i ^ mask) for i in range(size)])  28 us
    pallas_call x5, Pallas kernels, call(): pl.pallas_call(kernel, out_shape=out_shape, in_specs=[VMEM_SPEC] * len(op...  13.9 us
    ppermute x8, starting transfers between devices, exchange(): return lax.ppermute(array, 'seq', [(i, i ^ mask) for i in range(size)])  13.7 us
    unnamed x6, local copies, waits for them, and re-layouts  4.97 us
    concatenate x3, other arithmetic, shards(): window = jnp.concatenate([window, exchange(window, mask, peers)], axis=0)  2.52 us
  transfers between devices with their start and end apart: 8, of which 8 were waited for; matrix products, arithmetic and copies ran while one was open for 0% of the time, Pallas kernels for 0%

profile of v1, /device:TPU:0, one launch (start us, length us, event | category | flops | bytes accessed | tf_op | source)
XLA Modules:
  0.0 64.3 jit_solution(4150828613553194522)
XLA Ops:
  0.0 4.1 %collective-permute-start = (bf16[4,5120]{1,0:T(4,128)(2,1)}, bf16[4,5120]{1,0:T(4,128)(2,1)S(1)}, u32[]{:S(2)}, u32[]{:S(2)}) collective-permute-start(bf16[4,5120]{1,0:T(4,128)(2,1)} %param.4), channel_id=1, source_target_pairs={{0,8},{1,9},{2,10},{3,11},{4,12},{5,13},{6,14},{7,15},{8,0},{9,1},... | collective-permute-start | bytes 122888 | tf_op jit(solution)/shard_map/ppermute | solution.py:116
  4.1 2.6 %collective-permute-done = bf16[4,5120]{1,0:T(4,128)(2,1)S(1)} collective-permute-done((bf16[4,5120]{1,0:T(4,128)(2,1)}, bf16[4,5120]{1,0:T(4,128)(2,1)S(1)}, u32[]{:S(2)}, u32[]{:S(2)}) %collective-permute-start) | collective-permute-done | bytes 40992 | tf_op jit(solution)/shard_map/ppermute | solution.py:116
  6.7 0.8 %pad_maximum_fusion.2 = bf16[8,5120]{1,0:T(8,128)(2,1)S(1)} fusion(bf16[4,5120]{1,0:T(4,128)(2,1)S(1)} %collective-permute-done, bf16[4,5120]{1,0:T(4,128)(2,1)} %param.4), kind=kLoop, calls=%fused_computation.2 | loop fusion | flops 163840 | bytes 163840 | tf_op jit(solution)/shard_map/concatenate | solution.py:125
  7.5 1.5 %collective-permute-start.1 = (bf16[8,5120]{1,0:T(8,128)(2,1)S(1)}, bf16[8,5120]{1,0:T(8,128)(2,1)S(1)}, u32[]{:S(2)}, u32[]{:S(2)}) collective-permute-start(bf16[8,5120]{1,0:T(8,128)(2,1)S(1)} %pad_maximum_fusion.2), channel_id=1, source_target_pairs={{0,4},{1,5},{2,6},{3,7},{4,0},{5,1},{6,2},{7,3},{8,12},{9,13},{10,... | collective-permute-start | bytes 245768 | tf_op jit(solution)/shard_map/ppermute | solution.py:116
  9.1 3.0 %collective-permute-done.1 = bf16[8,5120]{1,0:T(8,128)(2,1)S(1)} collective-permute-done((bf16[8,5120]{1,0:T(8,128)(2,1)S(1)}, bf16[8,5120]{1,0:T(8,128)(2,1)S(1)}, u32[]{:S(2)}, u32[]{:S(2)}) %collective-permute-start.1) | collective-permute-done | bytes 81952 | tf_op jit(solution)/shard_map/ppermute | solution.py:116
  12.0 0.8 %pad_maximum_fusion.1 = bf16[16,5120]{1,0:T(8,128)(2,1)S(1)} fusion(bf16[8,5120]{1,0:T(8,128)(2,1)S(1)} %collective-permute-done.1, bf16[4,5120]{1,0:T(4,128)(2,1)S(1)} %collective-permute-done, bf16[4,5120]{1,0:T(4,128)(2,1)} %param.4), kind=kLoop, calls=%fused_computation.1 | loop fusion | flops 491520 | bytes 327680 | tf_op jit(solution)/shard_map/concatenate | solution.py:125
  12.9 1.8 %collective-permute-start.2 = (bf16[16,5120]{1,0:T(8,128)(2,1)S(1)}, bf16[16,5120]{1,0:T(8,128)(2,1)S(1)}, u32[]{:S(2)}, u32[]{:S(2)}) collective-permute-start(bf16[16,5120]{1,0:T(8,128)(2,1)S(1)} %pad_maximum_fusion.1), channel_id=1, source_target_pairs={{0,2},{1,3},{2,0},{3,1},{4,6},{5,7},{6,4},{7,5},{8,10},{9,11},{10,... | collective-permute-start | bytes 491528 | tf_op jit(solution)/shard_map/ppermute | solution.py:116
  14.7 3.6 %collective-permute-done.2 = bf16[16,5120]{1,0:T(8,128)(2,1)S(1)} collective-permute-done((bf16[16,5120]{1,0:T(8,128)(2,1)S(1)}, bf16[16,5120]{1,0:T(8,128)(2,1)S(1)}, u32[]{:S(2)}, u32[]{:S(2)}) %collective-permute-start.2) | collective-permute-done | bytes 163872 | tf_op jit(solution)/shard_map/ppermute | solution.py:116
  18.3 0.8 %pad_maximum_fusion = bf16[32,5120]{1,0:T(8,128)(2,1)S(1)} fusion(bf16[16,5120]{1,0:T(8,128)(2,1)S(1)} %collective-permute-done.2, bf16[8,5120]{1,0:T(8,128)(2,1)S(1)} %collective-permute-done.1, bf16[4,5120]{1,0:T(4,128)(2,1)S(1)} %collective-permute-done, bf16[4,5120]{1,0:T(4,128)(2,1)} %param.4), kind=kLoop, calls=%fused_computation | loop fusion | flops 1310720 | bytes 655360 | tf_op jit(solution)/shard_map/concatenate | solution.py:125
  19.2 1.6 %collective-permute-done.3 = bf16[32,5120]{1,0:T(8,128)(2,1)S(1)} collective-permute-done((bf16[32,5120]{1,0:T(8,128)(2,1)S(1)}, bf16[32,5120]{1,0:T(8,128)(2,1)S(1)}, u32[]{:S(2)}, u32[]{:S(2)}) %collective-permute-start.3) | collective-permute-done | bytes 327712 | tf_op jit(solution)/shard_map/ppermute | solution.py:116
  20.8 1.1 %concatenate.18.query_ref = bf16[64,5120]{1,0:T(8,128)(2,1)S(1)} concatenate(bf16[4,5120]{1,0:T(4,128)(2,1)} %param.4, bf16[4,5120]{1,0:T(4,128)(2,1)S(1)} %collective-permute-done, bf16[8,5120]{1,0:T(8,128)(2,1)S(1)} %collective-permute-done.1, bf16[16,5120]{1,0:T(8,128)(2,1)S(1)} %collective-permute-done.2, bf16[32,5120]{1,0:T(8,128)(2,1)S(1)} %collective-permute-done.3), dimensions={0} | concatenate | bytes 1310720 | tf_op jit(solution)/shard_map/concatenate | solution.py:125
  21.9 2.5 %copy-done = bf16[512,5120]{1,0:T(8,128)(2,1)S(1)} copy-done((bf16[512,5120]{1,0:T(8,128)(2,1)S(1)}, bf16[512,5120]{1,0:T(8,128)(2,1)}, u32[]{:S(2)}) %copy-start) | copy-done | bytes 5242904
  24.4 2.5 %copy-done.1 = bf16[512,5120]{1,0:T(8,128)(2,1)S(1)} copy-done((bf16[512,5120]{1,0:T(8,128)(2,1)S(1)}, bf16[512,5120]{1,0:T(8,128)(2,1)}, u32[]{:S(2)}) %copy-start.1) | copy-done | bytes 5242904
  26.8 12.0 %attend.1 = (f32[32,5376]{1,0:T(8,128)S(1)}, f32[32,5376]{1,0:T(8,128)S(1)}) custom-call(bf16[64,5120]{1,0:T(8,128)(2,1)S(1)} %concatenate.18.query_ref, bf16[512,5120]{1,0:T(8,128)(2,1)S(1)} %copy-done, bf16[512,5120]{1,0:T(8,128)(2,1)S(1)} %copy-done.1), custom_call_target="tpu_custom_call" | custom-call | flops 671088640 | bytes 12517376 | tf_op jit(solution)/shard_map/attend/pallas_call | solution.py:104
  39.1 2.0 %collective-permute-done.4.there_ref = f32[32,5376]{1,0:T(8,128)S(1)} collective-permute-done((f32[32,5376]{1,0:T(8,128)S(1)}, f32[32,5376]{1,0:T(8,128)S(1)}, u32[]{:S(2)}, u32[]{:S(2)}) %collective-permute-start.4) | collective-permute-done | bytes 688160 | tf_op jit(solution)/shard_map/ppermute | solution.py:116
  41.1 0.5 merge.3
  41.5 1.8 %collective-permute-start.5 = (f32[16,5376]{1,0:T(8,128)S(1)}, f32[16,5376]{1,0:T(8,128)S(1)}, u32[]{:S(2)}, u32[]{:S(2)}) collective-permute-start(f32[16,5376]{1,0:T(8,128)S(1)} %get-tuple-element.16), channel_id=1, source_target_pairs={{0,2},{1,3},{2,0},{3,1},{4,6},{5,7},{6,4},{7,5},{8,10},{9,11},{10,... | collective-permute-start | bytes 1032200 | tf_op jit(solution)/shard_map/ppermute | solution.py:116
  43.3 8.4 %collective-permute-done.5.there_ref = f32[16,5376]{1,0:T(8,128)S(1)} collective-permute-done((f32[16,5376]{1,0:T(8,128)S(1)}, f32[16,5376]{1,0:T(8,128)S(1)}, u32[]{:S(2)}, u32[]{:S(2)}) %collective-permute-start.5) | collective-permute-done | bytes 344096 | tf_op jit(solution)/shard_map/ppermute | solution.py:116
  51.7 0.3 merge.4
  52.0 1.5 %collective-permute-start.6 = (f32[8,5376]{1,0:T(8,128)S(1)}, f32[8,5376]{1,0:T(8,128)S(1)}, u32[]{:S(2)}, u32[]{:S(2)}) collective-permute-start(f32[8,5376]{1,0:T(8,128)S(1)} %get-tuple-element.18), channel_id=1, source_target_pairs={{0,4},{1,5},{2,6},{3,7},{4,0},{5,1},{6,2},{7,3},{8,12},{9,13},{10,... | collective-permute-start | bytes 516104 | tf_op jit(solution)/shard_map/ppermute | solution.py:116
  53.6 4.1 %collective-permute-done.6.there_ref = f32[8,5376]{1,0:T(8,128)S(1)} collective-permute-done((f32[8,5376]{1,0:T(8,128)S(1)}, f32[8,5376]{1,0:T(8,128)S(1)}, u32[]{:S(2)}, u32[]{:S(2)}) %collective-permute-start.6) | collective-permute-done | bytes 172064 | tf_op jit(solution)/shard_map/ppermute | solution.py:116
  57.9 2.7 %collective-permute-start.7 = (f32[4,5376]{1,0:T(4,128)S(1)}, f32[4,5376]{1,0:T(4,128)S(1)}, u32[]{:S(2)}, u32[]{:S(2)}) collective-permute-start(f32[4,5376]{1,0:T(4,128)S(1)} %get-tuple-element.20), channel_id=1, source_target_pairs={{0,8},{1,9},{2,10},{3,11},{4,12},{5,13},{6,14},{7,15},{8,0},{9,1},... | collective-permute-start | bytes 258056 | tf_op jit(solution)/shard_map/ppermute | solution.py:116
  60.6 2.8 %collective-permute-done.7.there_ref = f32[4,5376]{1,0:T(4,128)S(1)} collective-permute-done((f32[4,5376]{1,0:T(4,128)S(1)}, f32[4,5376]{1,0:T(4,128)S(1)}, u32[]{:S(2)}, u32[]{:S(2)}) %collective-permute-start.7) | collective-permute-done | bytes 86048 | tf_op jit(solution)/shard_map/ppermute | solution.py:116
  63.3 0.9 %finish.1 = bf16[4,5120]{1,0:T(4,128)(2,1)} custom-call(f32[4,5376]{1,0:T(4,128)S(1)} %get-tuple-element.19.here_ref, f32[4,5376]{1,0:T(4,128)S(1)} %collective-permute-done.7.there_ref, f32[1,5120]{1,0:T(1,128)S(1)} %bitcast.1), custom_call_target="tpu_custom_call" | custom-call | bytes 233472 | tf_op jit(solution)/shard_map/finish/pallas_call | solution.py:104
  (7 shorter events, 0.5 us)
Async XLA Ops:
  0.0 6.7 %collective-permute-start = (bf16[4,5120]{1,0:T(4,128)(2,1)}, bf16[4,5120]{1,0:T(4,128)(2,1)S(1)}, u32[]{:S(2)}, u32[]{:S(2)}) collective-permute-start(bf16[4,5120]{1,0:T(4,128)(2,1)} %param.4), channel_id=1, source_target_pairs={{0,8},{1,9},{2,10},{3,11},{4,12},{5,13},{6,14},{7,15},{8,0},{9,1},... | collective-permute-start | bytes 122888 | tf_op jit(solution)/shard_map/ppermute | solution.py:116
  7.5 4.5 %collective-permute-start.1 = (bf16[8,5120]{1,0:T(8,128)(2,1)S(1)}, bf16[8,5120]{1,0:T(8,128)(2,1)S(1)}, u32[]{:S(2)}, u32[]{:S(2)}) collective-permute-start(bf16[8,5120]{1,0:T(8,128)(2,1)S(1)} %pad_maximum_fusion.2), channel_id=1, source_target_pairs={{0,4},{1,5},{2,6},{3,7},{4,0},{5,1},{6,2},{7,3},{8,12},{9,13},{10,... | collective-permute-start | bytes 245768 | tf_op jit(solution)/shard_map/ppermute | solution.py:116
  12.9 5.4 %collective-permute-start.2 = (bf16[16,5120]{1,0:T(8,128)(2,1)S(1)}, bf16[16,5120]{1,0:T(8,128)(2,1)S(1)}, u32[]{:S(2)}, u32[]{:S(2)}) collective-permute-start(bf16[16,5120]{1,0:T(8,128)(2,1)S(1)} %pad_maximum_fusion.1), channel_id=1, source_target_pairs={{0,2},{1,3},{2,0},{3,1},{4,6},{5,7},{6,4},{7,5},{8,10},{9,11},{10,... | collective-permute-start | bytes 491528 | tf_op jit(solution)/shard_map/ppermute | solution.py:116
  19.1 1.7 %collective-permute-start.3 = (bf16[32,5120]{1,0:T(8,128)(2,1)S(1)}, bf16[32,5120]{1,0:T(8,128)(2,1)S(1)}, u32[]{:S(2)}, u32[]{:S(2)}) collective-permute-start(bf16[32,5120]{1,0:T(8,128)(2,1)S(1)} %pad_maximum_fusion), channel_id=1, source_target_pairs={{0,1},{1,0},{2,3},{3,2},{4,5},{5,4},{6,7},{7,6},{8,9},{9,8},{10,11... | collective-permute-start | bytes 983048 | tf_op jit(solution)/shard_map/ppermute | solution.py:116
  21.9 2.5 %copy-start = (bf16[512,5120]{1,0:T(8,128)(2,1)S(1)}, bf16[512,5120]{1,0:T(8,128)(2,1)}, u32[]{:S(2)}) copy-start(bf16[512,5120]{1,0:T(8,128)(2,1)} %key_ref.1) | copy-start | bytes 15728644
  24.4 2.5 %copy-start.1 = (bf16[512,5120]{1,0:T(8,128)(2,1)S(1)}, bf16[512,5120]{1,0:T(8,128)(2,1)}, u32[]{:S(2)}) copy-start(bf16[512,5120]{1,0:T(8,128)(2,1)} %value_ref.1) | copy-start | bytes 15728644
  26.8 36.5 %copy-start.2 = (f32[5120]{0:T(1024)S(1)}, f32[5120]{0:T(1024)}, u32[]{:S(2)}) copy-start(f32[5120]{0:T(1024)} %param.7) | copy-start | bytes 61444
  38.9 2.2 %collective-permute-start.4 = (f32[32,5376]{1,0:T(8,128)S(1)}, f32[32,5376]{1,0:T(8,128)S(1)}, u32[]{:S(2)}, u32[]{:S(2)}) collective-permute-start(f32[32,5376]{1,0:T(8,128)S(1)} %get-tuple-element.14), channel_id=1, source_target_pairs={{0,1},{1,0},{2,3},{3,2},{4,5},{5,4},{6,7},{7,6},{8,9},{9,8},{10,11... | collective-permute-start | bytes 2064392 | tf_op jit(solution)/shard_map/ppermute | solution.py:116
  41.5 10.2 %collective-permute-start.5 = (f32[16,5376]{1,0:T(8,128)S(1)}, f32[16,5376]{1,0:T(8,128)S(1)}, u32[]{:S(2)}, u32[]{:S(2)}) collective-permute-start(f32[16,5376]{1,0:T(8,128)S(1)} %get-tuple-element.16), channel_id=1, source_target_pairs={{0,2},{1,3},{2,0},{3,1},{4,6},{5,7},{6,4},{7,5},{8,10},{9,11},{10,... | collective-permute-start | bytes 1032200 | tf_op jit(solution)/shard_map/ppermute | solution.py:116
  52.0 5.6 %collective-permute-start.6 = (f32[8,5376]{1,0:T(8,128)S(1)}, f32[8,5376]{1,0:T(8,128)S(1)}, u32[]{:S(2)}, u32[]{:S(2)}) collective-permute-start(f32[8,5376]{1,0:T(8,128)S(1)} %get-tuple-element.18), channel_id=1, source_target_pairs={{0,4},{1,5},{2,6},{3,7},{4,0},{5,1},{6,2},{7,3},{8,12},{9,13},{10,... | collective-permute-start | bytes 516104 | tf_op jit(solution)/shard_map/ppermute | solution.py:116
  57.9 5.5 %collective-permute-start.7 = (f32[4,5376]{1,0:T(4,128)S(1)}, f32[4,5376]{1,0:T(4,128)S(1)}, u32[]{:S(2)}, u32[]{:S(2)}) collective-permute-start(f32[4,5376]{1,0:T(4,128)S(1)} %get-tuple-element.20), channel_id=1, source_target_pairs={{0,8},{1,9},{2,10},{3,11},{4,12},{5,13},{6,14},{7,15},{8,0},{9,1},... | collective-permute-start | bytes 258056 | tf_op jit(solution)/shard_map/ppermute | solution.py:116

commit v2 on v1

--- a/solution.py
+++ b/solution.py
@@ -9,6 +9,7 @@
 
 HDIM = 128
 EXP2_SCALE = math.log2(math.e) / math.sqrt(HDIM)
+FETCH_FLOPS = 6_000_000_000
 VMEM_SPEC = pl.BlockSpec(memory_space=pltpu.VMEM)
 
 
@@ -16,41 +17,53 @@
     return pl.ds(pl.multiple_of(head * HDIM, HDIM), HDIM)
 
 
-def attend_kernel(query_ref, key_ref, value_ref, keep_ref, send_ref):
-    rows, width = query_ref.shape
-    half = rows // 2
+def join_kernel(here_ref, there_ref, out_ref):
+    out_ref[...] = jnp.concatenate([here_ref[...], there_ref[...]], axis=0)
+
+
+def attend_kernel(query_here_ref, query_there_ref, key_ref, value_ref, keep_ref, send_ref, dots_ref, weights_ref):
+    half, width = query_here_ref.shape
+    rows = 2 * half
     heads = width // HDIM
-    lane = lax.broadcasted_iota(jnp.int32, (rows, HDIM), 1)
+    slots = dots_ref.shape[0]
 
-    def one_head(head, carry):
-        maxima, denominators = carry
-        columns = head_columns(head)
-        dots = lax.dot_general(
-            query_ref[:, columns],
+    def score(head):
+        columns = slice(head * HDIM, (head + 1) * HDIM)
+        dots_ref[head % slots] = lax.dot_general(
+            jnp.concatenate([query_here_ref[:, columns], query_there_ref[:, columns]], axis=0),
             key_ref[:, columns],
             (((1,), (1,)), ((), ())),
             preferred_element_type=jnp.float32,
         )
+
+    def weigh(head):
+        dots = dots_ref[head % slots]
         peak = jnp.max(dots, axis=1, keepdims=True)
         weights = jnp.exp2((dots - peak) * EXP2_SCALE)
         total = jnp.sum(weights, axis=1, keepdims=True)
         coarse = weights.astype(jnp.bfloat16)
-        fine = (weights - coarse.astype(jnp.float32)).astype(jnp.bfloat16)
-        sums = jnp.dot(
-            jnp.concatenate([coarse, fine], axis=0),
-            value_ref[:, columns],
-            preferred_element_type=jnp.float32,
-        )
+        weights_ref[head % slots, :rows] = coarse
+        weights_ref[head % slots, rows:] = (weights - coarse.astype(jnp.float32)).astype(jnp.bfloat16)
+        for ref, first in ((keep_ref, 0), (send_ref, half)):
+            ref[:, width + head : width + head + 1] = peak[first : first + half]
+            ref[:, width + HDIM + head : width + HDIM + head + 1] = total[first : first + half]
+
+    def accumulate(head):
+        columns = slice(head * HDIM, (head + 1) * HDIM)
+        sums = jnp.dot(weights_ref[head % slots], value_ref[:, columns], preferred_element_type=jnp.float32)
         numerator = sums[:rows] + sums[rows:]
         keep_ref[:, columns] = numerator[:half]
         send_ref[:, columns] = numerator[half:]
-        return jnp.where(lane == head, peak, maxima), jnp.where(lane == head, total, denominators)
 
-    zeros = jnp.zeros((rows, HDIM), jnp.float32)
-    maxima, denominators = lax.fori_loop(0, heads, one_head, (zeros, zeros), unroll=4)
-    for ref, first in ((keep_ref, 0), (send_ref, half)):
-        ref[:, width : width + HDIM] = maxima[first : first + half]
-        ref[:, width + HDIM :] = denominators[first : first + half]
+    group = slots // 2
+    for ref in (keep_ref, send_ref):
+        ref[:, width:] = jnp.zeros((half, 2 * HDIM), jnp.float32)
+    steps = heads // group
+    for step in range(steps + 2):
+        for member in range(group):
+            for stage, lag in ((score, 0), (weigh, 1), (accumulate, 2)):
+                if 0 <= step - lag < steps:
+                    stage((step - lag) * group + member)
 
 
 def merged_scales(here, there, width):
@@ -98,7 +111,7 @@
         out_ref[:, columns] = (block * inverse * gain_ref[:, columns]).astype(out_ref.dtype)
 
 
-def call(kernel, out_shape, operands, flops=0, name=None):
+def call(kernel, out_shape, operands, flops=0, name=None, scratch=(), limit=4 << 20):
     outs = out_shape if isinstance(out_shape, (tuple, list)) else [out_shape]
     size = sum(math.prod(a.shape) * a.dtype.itemsize for a in (*operands, *outs))
     return pl.pallas_call(
@@ -106,8 +119,9 @@
         out_shape=out_shape,
         in_specs=[VMEM_SPEC] * len(operands),
         out_specs=jax.tree.map(lambda _: VMEM_SPEC, out_shape),
+        scratch_shapes=scratch,
         cost_estimate=pl.CostEstimate(flops=flops, bytes_accessed=size, transcendentals=0),
-        compiler_params=pltpu.CompilerParams(vmem_limit_bytes=12 << 20),
+        compiler_params=pltpu.CompilerParams(vmem_limit_bytes=limit),
         name=name,
     )(*operands)
 
@@ -120,15 +134,27 @@
     peers = lax.axis_size("seq")
     masks = [1 << bit for bit in range(peers.bit_length() - 1)]
     rows, width = queries.shape
-    window = queries
+    tokens = keys.shape[0]
+    window, arrived = queries, None
     for mask in reversed(masks):
-        window = jnp.concatenate([window, exchange(window, mask, peers)], axis=0)
+        if arrived is not None:
+            both = jax.ShapeDtypeStruct((2 * window.shape[0], width), window.dtype)
+            window = call(join_kernel, both, (window, arrived), FETCH_FLOPS, "join")
+        arrived = exchange(window, mask, peers)
+    count = 2 * window.shape[0]
 
     def pair(count):
         return (jax.ShapeDtypeStruct((count, width + 2 * HDIM), jnp.float32),) * 2
 
-    flops = 4 * window.shape[0] * keys.shape[0] * width
-    keep, send = call(attend_kernel, pair(window.shape[0] // 2), (window, keys, values), flops, "attend")
+    keep, send = call(
+        attend_kernel,
+        pair(count // 2),
+        (window, arrived, keys, values),
+        4 * count * tokens * width,
+        "attend",
+        [pltpu.VMEM((4, count, tokens), jnp.float32), pltpu.VMEM((4, 2 * count, tokens), jnp.bfloat16)],
+        16 << 20,
+    )
     for mask in masks[:-1]:
         arrived = exchange(send, mask, peers)
         keep, send = call(merge_kernel, pair(keep.shape[0] // 2), (keep, arrived), 0, "merge")

time: 64.7 us -> 48.4 us (0.75)
  Pallas kernels: 13.9 us -> 5.59 us
  local copies, waits for them, and re-layouts: 6.02 us -> 0.81 us
  other arithmetic: 2.52 us -> 0.01 us
    pallas_call x5 -> x8, Pallas kernels: 13.9 us -> 5.59 us  [call(): pl.pallas_call(kernel, out_shape=out_shape, in_specs=[VMEM_SPEC] * len(op...]
    unnamed x6 -> x12, local copies, waits for them, and re-layouts: 4.97 us -> 0.81 us
    concatenate x3 -> x0, other arithmetic: 2.52 us -> none  [shards(): window = jnp.concatenate([window, exchange(window, mask, peers)], axis=0)]
    concatenate x1 -> x0, local copies, waits for them, and re-layouts: 1.05 us -> none  [shards(): window = jnp.concatenate([window, exchange(window, mask, peers)], axis=0)]
where the time goes in v2:
time: 48.4 us; the launch traced here: 48.2 us
  waiting for transfers between devices  28 us (58%)
  starting transfers between devices  13.7 us (28%)
  Pallas kernels  5.59 us (12%)
  local copies, waits for them, and re-layouts  0.81 us (2%)
    ppermute x8, waiting for transfers between devices, exchange(): return lax.ppermute(array, 'seq', [(i, i ^ mask) for i in range(size)])  28 us
    ppermute x8, starting transfers between devices, exchange(): return lax.ppermute(array, 'seq', [(i, i ^ mask) for i in range(size)])  13.7 us
    pallas_call x8, Pallas kernels, call(): pl.pallas_call(kernel, out_shape=out_shape, in_specs=[VMEM_SPEC] * len(op...  5.59 us
  transfers between devices with their start and end apart: 8, of which 8 were waited for; matrix products, arithmetic and copies ran while one was open for 0% of the time, Pallas kernels for 0%

profile of v2, /device:TPU:0, one launch (start us, length us, event | category | flops | bytes accessed | tf_op | source)
XLA Modules:
  0.0 48.2 jit_solution(2693796120900626846)
XLA Ops:
  0.0 4.1 %collective-permute-start = (bf16[4,5120]{1,0:T(4,128)(2,1)}, bf16[4,5120]{1,0:T(4,128)(2,1)S(1)}, u32[]{:S(2)}, u32[]{:S(2)}) collective-permute-start(bf16[4,5120]{1,0:T(4,128)(2,1)} %here_ref.1), channel_id=1, source_target_pairs={{0,8},{1,9},{2,10},{3,11},{4,12},{5,13},{6,14},{7,15},{8,0},{9,1},... | collective-permute-start | bytes 122888 | tf_op jit(solution)/shard_map/ppermute | solution.py:130
  4.1 2.6 %collective-permute-done.there_ref = bf16[4,5120]{1,0:T(4,128)(2,1)S(1)} collective-permute-done((bf16[4,5120]{1,0:T(4,128)(2,1)}, bf16[4,5120]{1,0:T(4,128)(2,1)S(1)}, u32[]{:S(2)}, u32[]{:S(2)}) %collective-permute-start) | collective-permute-done | bytes 40992 | tf_op jit(solution)/shard_map/ppermute | solution.py:130
  6.7 0.8 %copy-done.1 = bf16[4,5120]{1,0:T(4,128)(2,1)S(1)} copy-done((bf16[4,5120]{1,0:T(4,128)(2,1)S(1)}, bf16[4,5120]{1,0:T(4,128)(2,1)}, u32[]{:S(2)}) %copy-start.1) | copy-done | bytes 40984
  7.5 1.5 %collective-permute-start.1 = (bf16[8,5120]{1,0:T(8,128)(2,1)S(1)}, bf16[8,5120]{1,0:T(8,128)(2,1)S(1)}, u32[]{:S(2)}, u32[]{:S(2)}) collective-permute-start(bf16[8,5120]{1,0:T(8,128)(2,1)S(1)} %join.3.here_ref), channel_id=1, source_target_pairs={{0,4},{1,5},{2,6},{3,7},{4,0},{5,1},{6,2},{7,3},{8,12},{9,13},{10,... | collective-permute-start | bytes 245768 | tf_op jit(solution)/shard_map/ppermute | solution.py:130
  9.0 3.0 %collective-permute-done.1.there_ref = bf16[8,5120]{1,0:T(8,128)(2,1)S(1)} collective-permute-done((bf16[8,5120]{1,0:T(8,128)(2,1)S(1)}, bf16[8,5120]{1,0:T(8,128)(2,1)S(1)}, u32[]{:S(2)}, u32[]{:S(2)}) %collective-permute-start.1) | collective-permute-done | bytes 81952 | tf_op jit(solution)/shard_map/ppermute | solution.py:130
  12.0 0.0 slice-start.1
  12.1 0.0 slice-start.3
  12.1 1.8 %collective-permute-start.2 = (bf16[16,5120]{1,0:T(8,128)(2,1)S(1)}, bf16[16,5120]{1,0:T(8,128)(2,1)S(1)}, u32[]{:S(2)}, u32[]{:S(2)}) collective-permute-start(bf16[16,5120]{1,0:T(8,128)(2,1)S(1)} %join.4.here_ref), channel_id=1, source_target_pairs={{0,2},{1,3},{2,0},{3,1},{4,6},{5,7},{6,4},{7,5},{8,10},{9,11},{10,... | collective-permute-start | bytes 491528 | tf_op jit(solution)/shard_map/ppermute | solution.py:130
  13.9 3.6 %collective-permute-done.2.there_ref = bf16[16,5120]{1,0:T(8,128)(2,1)S(1)} collective-permute-done((bf16[16,5120]{1,0:T(8,128)(2,1)S(1)}, bf16[16,5120]{1,0:T(8,128)(2,1)S(1)}, u32[]{:S(2)}, u32[]{:S(2)}) %collective-permute-start.2) | collective-permute-done | bytes 163872 | tf_op jit(solution)/shard_map/ppermute | solution.py:130
  17.5 0.1 collective-permute-start.3
  17.6 1.6 %collective-permute-done.3.query_there_ref = bf16[32,5120]{1,0:T(8,128)(2,1)S(1)} collective-permute-done((bf16[32,5120]{1,0:T(8,128)(2,1)S(1)}, bf16[32,5120]{1,0:T(8,128)(2,1)S(1)}, u32[]{:S(2)}, u32[]{:S(2)}) %collective-permute-start.3) | collective-permute-done | bytes 327712 | tf_op jit(solution)/shard_map/ppermute | solution.py:130
  19.2 3.6 %attend.1 = (f32[32,5376]{1,0:T(8,128)S(1)}, f32[32,5376]{1,0:T(8,128)S(1)}) custom-call(bf16[32,5120]{1,0:T(8,128)(2,1)S(1)} %join.5.query_here_ref, bf16[32,5120]{1,0:T(8,128)(2,1)S(1)} %collective-permute-done.3.query_there_ref, bf16[512,5120]{1,0:T(8,128)(2,1)S(1)} %bitcast.2, bf16[512,5120]{1,0:T(8,128)(2,1)S(1)} %bitcast.4), custom_call_target="tpu_custom_call" | custom-call | flops 671088640 | bytes 12517376 | tf_op jit(solution)/shard_map/attend/pallas_call | solution.py:117
  22.8 0.2 collective-permute-start.4
  23.0 2.0 %collective-permute-done.4.there_ref = f32[32,5376]{1,0:T(8,128)S(1)} collective-permute-done((f32[32,5376]{1,0:T(8,128)S(1)}, f32[32,5376]{1,0:T(8,128)S(1)}, u32[]{:S(2)}, u32[]{:S(2)}) %collective-permute-start.4) | collective-permute-done | bytes 688160 | tf_op jit(solution)/shard_map/ppermute | solution.py:130
  25.0 0.5 merge.3
  25.5 1.8 %collective-permute-start.5 = (f32[16,5376]{1,0:T(8,128)S(1)}, f32[16,5376]{1,0:T(8,128)S(1)}, u32[]{:S(2)}, u32[]{:S(2)}) collective-permute-start(f32[16,5376]{1,0:T(8,128)S(1)} %get-tuple-element.16), channel_id=1, source_target_pairs={{0,2},{1,3},{2,0},{3,1},{4,6},{5,7},{6,4},{7,5},{8,10},{9,11},{10,... | collective-permute-start | bytes 1032200 | tf_op jit(solution)/shard_map/ppermute | solution.py:130
  27.3 8.4 %collective-permute-done.5.there_ref = f32[16,5376]{1,0:T(8,128)S(1)} collective-permute-done((f32[16,5376]{1,0:T(8,128)S(1)}, f32[16,5376]{1,0:T(8,128)S(1)}, u32[]{:S(2)}, u32[]{:S(2)}) %collective-permute-start.5) | collective-permute-done | bytes 344096 | tf_op jit(solution)/shard_map/ppermute | solution.py:130
  35.7 0.3 merge.4
  36.0 1.5 %collective-permute-start.6 = (f32[8,5376]{1,0:T(8,128)S(1)}, f32[8,5376]{1,0:T(8,128)S(1)}, u32[]{:S(2)}, u32[]{:S(2)}) collective-permute-start(f32[8,5376]{1,0:T(8,128)S(1)} %get-tuple-element.18), channel_id=1, source_target_pairs={{0,4},{1,5},{2,6},{3,7},{4,0},{5,1},{6,2},{7,3},{8,12},{9,13},{10,... | collective-permute-start | bytes 516104 | tf_op jit(solution)/shard_map/ppermute | solution.py:130
  37.5 4.1 %collective-permute-done.6.there_ref = f32[8,5376]{1,0:T(8,128)S(1)} collective-permute-done((f32[8,5376]{1,0:T(8,128)S(1)}, f32[8,5376]{1,0:T(8,128)S(1)}, u32[]{:S(2)}, u32[]{:S(2)}) %collective-permute-start.6) | collective-permute-done | bytes 172064 | tf_op jit(solution)/shard_map/ppermute | solution.py:130
  41.6 0.2 merge.5
  41.8 2.7 %collective-permute-start.7 = (f32[4,5376]{1,0:T(4,128)S(1)}, f32[4,5376]{1,0:T(4,128)S(1)}, u32[]{:S(2)}, u32[]{:S(2)}) collective-permute-start(f32[4,5376]{1,0:T(4,128)S(1)} %get-tuple-element.20), channel_id=1, source_target_pairs={{0,8},{1,9},{2,10},{3,11},{4,12},{5,13},{6,14},{7,15},{8,0},{9,1},... | collective-permute-start | bytes 258056 | tf_op jit(solution)/shard_map/ppermute | solution.py:130
  44.5 2.7 %collective-permute-done.7.there_ref = f32[4,5376]{1,0:T(4,128)S(1)} collective-permute-done((f32[4,5376]{1,0:T(4,128)S(1)}, f32[4,5376]{1,0:T(4,128)S(1)}, u32[]{:S(2)}, u32[]{:S(2)}) %collective-permute-start.7) | collective-permute-done | bytes 86048 | tf_op jit(solution)/shard_map/ppermute | solution.py:130
  47.3 0.9 %finish.1 = bf16[4,5120]{1,0:T(4,128)(2,1)} custom-call(f32[4,5376]{1,0:T(4,128)S(1)} %get-tuple-element.19.here_ref, f32[4,5376]{1,0:T(4,128)S(1)} %collective-permute-done.7.there_ref, f32[1,5120]{1,0:T(1,128)S(1)} %bitcast.5), custom_call_target="tpu_custom_call" | custom-call | bytes 233472 | tf_op jit(solution)/shard_map/finish/pallas_call | solution.py:117
  (14 shorter events, 0.1 us)
Async XLA Ops:
  0.0 6.7 %collective-permute-start = (bf16[4,5120]{1,0:T(4,128)(2,1)}, bf16[4,5120]{1,0:T(4,128)(2,1)S(1)}, u32[]{:S(2)}, u32[]{:S(2)}) collective-permute-start(bf16[4,5120]{1,0:T(4,128)(2,1)} %here_ref.1), channel_id=1, source_target_pairs={{0,8},{1,9},{2,10},{3,11},{4,12},{5,13},{6,14},{7,15},{8,0},{9,1},... | collective-permute-start | bytes 122888 | tf_op jit(solution)/shard_map/ppermute | solution.py:130
  6.7 0.8 %copy-start.1 = (bf16[4,5120]{1,0:T(4,128)(2,1)S(1)}, bf16[4,5120]{1,0:T(4,128)(2,1)}, u32[]{:S(2)}) copy-start(bf16[4,5120]{1,0:T(4,128)(2,1)} %here_ref.1) | copy-start | bytes 122884
  7.5 4.5 %collective-permute-start.1 = (bf16[8,5120]{1,0:T(8,128)(2,1)S(1)}, bf16[8,5120]{1,0:T(8,128)(2,1)S(1)}, u32[]{:S(2)}, u32[]{:S(2)}) collective-permute-start(bf16[8,5120]{1,0:T(8,128)(2,1)S(1)} %join.3.here_ref), channel_id=1, source_target_pairs={{0,4},{1,5},{2,6},{3,7},{4,0},{5,1},{6,2},{7,3},{8,12},{9,13},{10,... | collective-permute-start | bytes 245768 | tf_op jit(solution)/shard_map/ppermute | solution.py:130
  12.0 7.2 %slice-start = ((s8[5242880]{0:T(1024)(128)(4,1)}), s8[4194304]{0:T(1024)(128)(4,1)S(1)}, s32[]{:S(2)}) async-start(s8[5242880]{0:T(1024)(128)(4,1)} %bitcast.1), calls=%async_computation | async-start | bytes 8388608
  12.0 7.2 %slice-start.2 = ((s8[5242880]{0:T(1024)(128)(4,1)}), s8[4194304]{0:T(1024)(128)(4,1)S(1)}, s32[]{:S(2)}) async-start(s8[5242880]{0:T(1024)(128)(4,1)} %bitcast.3), calls=%async_computation.2 | async-start | bytes 8388608
  12.0 7.2 %slice-start.1 = ((s8[5242880]{0:T(1024)(128)(4,1)}), s8[1048576]{0:T(1024)(128)(4,1)S(1)}, s32[]{:S(2)}) async-start(s8[5242880]{0:T(1024)(128)(4,1)} %bitcast.1), calls=%async_computation.1 | async-start | bytes 2097152
  12.1 7.1 %slice-start.3 = ((s8[5242880]{0:T(1024)(128)(4,1)}), s8[1048576]{0:T(1024)(128)(4,1)S(1)}, s32[]{:S(2)}) async-start(s8[5242880]{0:T(1024)(128)(4,1)} %bitcast.3), calls=%async_computation.3 | async-start | bytes 2097152
  12.1 5.4 %collective-permute-start.2 = (bf16[16,5120]{1,0:T(8,128)(2,1)S(1)}, bf16[16,5120]{1,0:T(8,128)(2,1)S(1)}, u32[]{:S(2)}, u32[]{:S(2)}) collective-permute-start(bf16[16,5120]{1,0:T(8,128)(2,1)S(1)} %join.4.here_ref), channel_id=1, source_target_pairs={{0,2},{1,3},{2,0},{3,1},{4,6},{5,7},{6,4},{7,5},{8,10},{9,11},{10,... | collective-permute-start | bytes 491528 | tf_op jit(solution)/shard_map/ppermute | solution.py:130
  17.5 29.8 %copy-start = (f32[5120]{0:T(1024)S(1)}, f32[5120]{0:T(1024)}, u32[]{:S(2)}) copy-start(f32[5120]{0:T(1024)} %param.7) | copy-start | bytes 61444
  17.5 1.7 %collective-permute-start.3 = (bf16[32,5120]{1,0:T(8,128)(2,1)S(1)}, bf16[32,5120]{1,0:T(8,128)(2,1)S(1)}, u32[]{:S(2)}, u32[]{:S(2)}) collective-permute-start(bf16[32,5120]{1,0:T(8,128)(2,1)S(1)} %join.5.query_here_ref), channel_id=1, source_target_pairs={{0,1},{1,0},{2,3},{3,2},{4,5},{5,4},{6,7},{7,6},{8,9},{9,8},{10,11... | collective-permute-start | bytes 983048 | tf_op jit(solution)/shard_map/ppermute | solution.py:130
  22.8 2.2 %collective-permute-start.4 = (f32[32,5376]{1,0:T(8,128)S(1)}, f32[32,5376]{1,0:T(8,128)S(1)}, u32[]{:S(2)}, u32[]{:S(2)}) collective-permute-start(f32[32,5376]{1,0:T(8,128)S(1)} %get-tuple-element.14), channel_id=1, source_target_pairs={{0,1},{1,0},{2,3},{3,2},{4,5},{5,4},{6,7},{7,6},{8,9},{9,8},{10,11... | collective-permute-start | bytes 2064392 | tf_op jit(solution)/shard_map/ppermute | solution.py:130
  25.5 10.2 %collective-permute-start.5 = (f32[16,5376]{1,0:T(8,128)S(1)}, f32[16,5376]{1,0:T(8,128)S(1)}, u32[]{:S(2)}, u32[]{:S(2)}) collective-permute-start(f32[16,5376]{1,0:T(8,128)S(1)} %get-tuple-element.16), channel_id=1, source_target_pairs={{0,2},{1,3},{2,0},{3,1},{4,6},{5,7},{6,4},{7,5},{8,10},{9,11},{10,... | collective-permute-start | bytes 1032200 | tf_op jit(solution)/shard_map/ppermute | solution.py:130
  36.0 5.6 %collective-permute-start.6 = (f32[8,5376]{1,0:T(8,128)S(1)}, f32[8,5376]{1,0:T(8,128)S(1)}, u32[]{:S(2)}, u32[]{:S(2)}) collective-permute-start(f32[8,5376]{1,0:T(8,128)S(1)} %get-tuple-element.18), channel_id=1, source_target_pairs={{0,4},{1,5},{2,6},{3,7},{4,0},{5,1},{6,2},{7,3},{8,12},{9,13},{10,... | collective-permute-start | bytes 516104 | tf_op jit(solution)/shard_map/ppermute | solution.py:130
  41.8 5.5 %collective-permute-start.7 = (f32[4,5376]{1,0:T(4,128)S(1)}, f32[4,5376]{1,0:T(4,128)S(1)}, u32[]{:S(2)}, u32[]{:S(2)}) collective-permute-start(f32[4,5376]{1,0:T(4,128)S(1)} %get-tuple-element.20), channel_id=1, source_target_pairs={{0,8},{1,9},{2,10},{3,11},{4,12},{5,13},{6,14},{7,15},{8,0},{9,1},... | collective-permute-start | bytes 258056 | tf_op jit(solution)/shard_map/ppermute | solution.py:130
